TPU v7x, 32 devices: a whole 2x2x4 slice. The times are simulated.
32 devices in a mesh: seq: 4 (over z), tensor: 2 (over y), section: 4 (over x, core).
Axes of the slice: x: 2, y: 2, z: 4, core: 2. Of those that a mesh axis runs over, the one named last changes fastest.
Arguments:
- dec_inputs: bfloat16 [4, 1024, 4096], P('section', 'seq'), may hold values from -64 to 64
- w_query: bfloat16 [4, 4096, 512], P('section', None, 'tensor')
- w_key: bfloat16 [4, 4096, 512], P('section', None, 'tensor')
- w_value: bfloat16 [4, 4096, 512], P('section', None, 'tensor'), may hold values from -0.09375 to 0.09375
- ctx_grad: bfloat16 [4, 1024, 512], P('section', 'seq', 'tensor'), may hold values from -96 to 96
- encoded: bfloat16 [448, 4096], P('seq'), may hold values from -11 to 11
- enc_lengths: int32 [4], replicated, may hold values from 0 to 112, as said below
Outputs:
- dec_grad: bfloat16 [4, 1024, 4096], P('section', 'seq', 'tensor')
- enc_grad: bfloat16 [448, 4096], P('seq', ('tensor', 'section'))
Inputs may be any that keep to these rules, and one draw needn't show every extreme that they name: `enc_lengths`: each block holds a prefix of valid tokens; in every draw some block is wholly valid and blocks may be empty.
All inputs are finite; a program needn't handle non-finite values.
Results may differ from a plain program's by a relative error of at most 0.018.
Values may be sent and summed in bfloat16 or wider, within the bound.
A program may use at most 64 MiB of HBM per device.

v0:
```python
import math

import jax
import jax.numpy as jnp
from jax import lax
from jax.sharding import PartitionSpec as P

masked_fill = -1e30


def body(dec_inputs, w_query, w_key, w_value, ctx_grad, encoded, enc_lengths):
    inputs = dec_inputs[0]
    wq_own = w_query[0]
    wk_own = w_key[0]
    wv_own = w_value[0]
    dout = ctx_grad[0]
    scale = 1.0 / math.sqrt(wq_own.shape[1])
    blocks = enc_lengths.shape[0]
    kdev = encoded.shape[0]
    query = jnp.dot(inputs, wq_own, preferred_element_type=jnp.float32).astype(jnp.bfloat16)
    key = jnp.dot(encoded, wk_own, preferred_element_type=jnp.float32).astype(jnp.bfloat16)
    value = jnp.dot(encoded, wv_own, preferred_element_type=jnp.float32).astype(jnp.bfloat16)
    key_all, value_all = (
        lax.all_gather(key, "seq", axis=0, tiled=True),
        lax.all_gather(value, "seq", axis=0, tiled=True),
    )
    limit = jnp.broadcast_to(enc_lengths[:, None], (blocks, kdev)).reshape(-1)
    slots = lax.broadcasted_iota(jnp.int32, (blocks, kdev), 1).reshape(-1)
    valid = (slots < limit)[None, :]
    scores = jnp.einsum("qd,kd->qk", query, key_all, preferred_element_type=jnp.float32) * scale
    scores = jnp.where(valid, scores, masked_fill)
    top = jnp.max(scores, axis=1, keepdims=True)
    expd = jnp.where(valid, jnp.exp(scores - top), 0.0)
    probs = expd / jnp.sum(expd, axis=1, keepdims=True)
    dprob = jnp.einsum("qd,kd->qk", dout, value_all, preferred_element_type=jnp.float32)
    delta = jnp.sum(probs * dprob, axis=1, keepdims=True)
    dscore = (probs * (dprob - delta) * scale).astype(jnp.bfloat16)
    probs_b = probs.astype(jnp.bfloat16)
    dquery = jnp.dot(dscore, key_all, preferred_element_type=jnp.float32).astype(jnp.bfloat16)
    dkey_part = jnp.einsum("qk,qd->kd", dscore, query, preferred_element_type=jnp.float32)
    dvalue_part = jnp.einsum("qk,qd->kd", probs_b, dout, preferred_element_type=jnp.float32)
    dkey_sum, dvalue_sum = (
        lax.psum_scatter(
            dkey_part.astype(jnp.bfloat16), "seq", scatter_dimension=0, tiled=True
        ).astype(jnp.float32),
        lax.psum_scatter(
            dvalue_part.astype(jnp.bfloat16), "seq", scatter_dimension=0, tiled=True
        ).astype(jnp.float32),
    )
    dkey = dkey_sum.astype(jnp.bfloat16)
    dvalue = dvalue_sum.astype(jnp.bfloat16)
    input_term = jnp.einsum("qd,ed->qe", dquery, wq_own, preferred_element_type=jnp.float32)
    dec_grad = lax.psum_scatter(
        input_term.astype(jnp.bfloat16), "tensor", scatter_dimension=1, tiled=True
    )
    encoder_term = jnp.einsum("kd,ed->ke", dkey, wk_own, preferred_element_type=jnp.float32)
    encoder_term = encoder_term + jnp.einsum(
        "kd,ed->ke", dvalue, wv_own, preferred_element_type=jnp.float32
    )
    enc_grad = lax.psum_scatter(
        encoder_term.astype(jnp.bfloat16), ("tensor", "section"), scatter_dimension=1, tiled=True
    )
    return (dec_grad[None, :, :], enc_grad)


def solution(mesh):
    in_specs = (
        P("section", "seq", None),
        P("section", None, "tensor"),
        P("section", None, "tensor"),
        P("section", None, "tensor"),
        P("section", "seq", "tensor"),
        P("seq", None),
        P(),
    )
    out_specs = (P("section", "seq", "tensor"), P("seq", ("tensor", "section")))
    return jax.shard_map(body, mesh=mesh, in_specs=in_specs, out_specs=out_specs, check_vma=False)
```

profile of v0, /device:TPU:0, one launch (start us, length us, event | category | flops | bytes accessed | tf_op | source)
XLA Modules:
  0.0 163.3 jit_solution(12802926421233766787)
XLA Ops:
  7.2 0.0 copy-start
  7.2 0.0 copy-start.2
  7.2 0.0 reduce-scatter.7.cloned.1.call-start
  7.2 0.9 iota_compare_fusion
  8.1 0.1 lt.11
  8.2 0.0 copy-start.1
  8.2 2.5 %fusion.18 = bf16[112,256]{1,0:T(8,128)(2,1)S(1)} fusion(bf16[112,4096]{1,0:T(8,128)(2,1)} %param.12, bf16[1,4096,256]{2,1,0:T(8,128)(2,1)} %param.9), kind=kOutput, calls=%fused_computation.21 | convolution fusion | flops 234909696 | bytes 3072000 | tf_op jit(solution)/shard_map/dot_general | solution.py:21
  10.7 0.0 copy-start.3
  10.7 15.6 %all_gather.6 = bf16[448,256]{1,0:T(8,128)(2,1)S(1)} all-gather(bf16[112,256]{1,0:T(8,128)(2,1)S(1)} %fusion.18), channel_id=1, replica_groups=mesh['seq'=4,'tensor'=2,'section'=4] {'seq'}, dimensions={0}, use_global_device_ids=true | all-gather | bytes 286720 | tf_op jit(solution)/shard_map/all_gather | solution.py:24
  26.4 0.0 copy-done.2
  26.4 0.0 copy-done.1
  26.4 0.4 fusion.21
  26.8 14.2 %all_gather.7 = bf16[448,256]{1,0:T(8,128)(2,1)S(1)} all-gather(bf16[112,256]{1,0:T(8,128)(2,1)S(1)} %fusion.21), channel_id=1, replica_groups=mesh['seq'=4,'tensor'=2,'section'=4] {'seq'}, dimensions={0}, use_global_device_ids=true | all-gather | bytes 286720 | tf_op jit(solution)/shard_map/all_gather | solution.py:25
  41.0 0.0 copy-done
  41.0 0.0 copy-done.3
  41.0 0.0 copy-start.4
  41.0 0.7 fusion.13
  41.7 0.3 fusion.30
  42.0 0.1 fusion.25
  42.2 0.0 copy-done.4
  42.2 0.3 multiply_reduce_fusion
  42.5 0.2 multiply_convert_fusion
  42.7 0.9 convolution_convert_fusion.2
  43.6 0.0 reduce-scatter.7.cloned.1.call-update
  43.6 0.0 reduce-scatter.9.cloned.1.call-start
  43.7 1.0 convolution_convert_fusion.1
  44.6 0.0 reduce-scatter.9.cloned.1.call-update
  44.6 0.0 reduce-scatter.11.cloned.1.call-start
  44.7 19.7 %reduce-scatter.7.cloned.1.call-done = bf16[112,256]{1,0:T(8,128)(2,1)} async-done(((bf16[448,256]{1,0:T(8,128)(2,1)}), bf16[112,256]{1,0:T(8,128)(2,1)}) %reduce-scatter.7.cloned.1.call-update) | async-done | bytes 57360 | tf_op jit(solution)/shard_map/reduce_scatter | solution.py:43
  64.4 3.7 %fusion.4 = f32[112,4096]{1,0:T(8,128)} fusion(bf16[112,256]{1,0:T(8,128)(2,1)} %reduce-scatter.7.cloned.1.call-done, bf16[1,4096,256]{2,1,0:T(8,128)(2,1)} %param.9), kind=kOutput, calls=%fused_computation.6 | convolution fusion | flops 234881024 | bytes 3989504 | tf_op jit(solution)/shard_map/kd,ed->ke/dot_general | solution.py:56
  68.1 16.5 %reduce-scatter.9.cloned.1.call-done = bf16[112,256]{1,0:T(8,128)(2,1)} async-done(((bf16[448,256]{1,0:T(8,128)(2,1)}), bf16[112,256]{1,0:T(8,128)(2,1)}) %reduce-scatter.9.cloned.1.call-update) | async-done | bytes 57360 | tf_op jit(solution)/shard_map/reduce_scatter | solution.py:46
  84.6 3.9 %fusion = bf16[112,4096]{1,0:T(8,128)(2,1)} fusion(f32[112,4096]{1,0:T(8,128)} %fusion.4, bf16[112,256]{1,0:T(8,128)(2,1)} %reduce-scatter.9.cloned.1.call-done, bf16[1,4096,256]{2,1,0:T(8,128)(2,1)} %param.10), kind=kOutput, calls=%fused_computation.2 | convolution fusion | flops 235798528 | bytes 4907008 | tf_op jit(solution)/shard_map/kd,ed->ke/dot_general | solution.py:57
  88.4 0.0 reduce-scatter.11.cloned.1.call-update
  88.5 0.0 reduce-scatter.5.cloned.1.call-start
  88.5 2.3 %convolution_convert_fusion = bf16[256,4096]{1,0:T(8,128)(2,1)} fusion(bf16[1,4096,256]{2,1,0:T(8,128)(2,1)S(1)} %copy-done, bf16[256,448]{0,1:T(8,128)(2,1)S(1)} %multiply_convert_fusion, bf16[448,256]{1,0:T(8,128)(2,1)S(1)} %all_gather.6), kind=kOutput, calls=%fused_computation | convolution fusion | flops 596705280 | bytes 4653056 | tf_op jit(solution)/shard_map/qd,ed->qe/dot_general | solution.py:52
  90.8 0.0 reduce-scatter.5.cloned.1.call-update
  90.9 31.5 %reduce-scatter.11.cloned.1.call-done = bf16[112,512]{1,0:T(8,128)(2,1)} async-done(((bf16[112,4096]{1,0:T(8,128)(2,1)}), bf16[112,512]{1,0:T(8,128)(2,1)}) %reduce-scatter.11.cloned.1.call-update) | async-done | bytes 114704 | tf_op jit(solution)/shard_map/reduce_scatter | solution.py:60
  122.3 34.5 %reduce-scatter.5.cloned.1.call-done = bf16[256,2048]{1,0:T(8,128)(2,1)} async-done(((bf16[256,4096]{1,0:T(8,128)(2,1)}), bf16[256,2048]{1,0:T(8,128)(2,1)}) %reduce-scatter.5.cloned.1.call-update) | async-done | bytes 1048592 | tf_op jit(solution)/shard_map/reduce_scatter | solution.py:53
Async XLA Ops:
  7.2 33.8 %copy-start = (bf16[1,4096,256]{2,1,0:T(8,128)(2,1)S(1)}, bf16[1,4096,256]{2,1,0:T(8,128)(2,1)}, u32[]{:S(2)}) copy-start(bf16[1,4096,256]{2,1,0:T(8,128)(2,1)} %param.8) | copy-start | bytes 6291460
  7.2 19.2 %copy-start.2 = (bf16[112,4096]{1,0:T(8,128)(2,1)S(1)}, bf16[112,4096]{1,0:T(8,128)(2,1)}, u32[]{:S(2)}) copy-start(bf16[112,4096]{1,0:T(8,128)(2,1)} %param.12) | copy-start | bytes 2752516
  7.2 57.2 %reduce-scatter.7.cloned.1.call-start = ((), (), s32[]{:S(2)}) async-start(), calls=%async_computation.5 | async-start | bytes 286720 | tf_op jit(solution)/shard_map/reduce_scatter | solution.py:43
  8.2 18.1 %copy-start.1 = (bf16[1,4096,256]{2,1,0:T(8,128)(2,1)S(1)}, bf16[1,4096,256]{2,1,0:T(8,128)(2,1)}, u32[]{:S(2)}) copy-start(bf16[1,4096,256]{2,1,0:T(8,128)(2,1)} %param.10) | copy-start | bytes 6291460
  10.7 30.3 %copy-start.3 = (bf16[1,256,4096]{2,1,0:T(8,128)(2,1)S(1)}, bf16[1,256,4096]{2,1,0:T(8,128)(2,1)}, u32[]{:S(2)}) copy-start(bf16[1,256,4096]{2,1,0:T(8,128)(2,1)} %param.7) | copy-start | bytes 6291460
  41.0 1.2 copy-start.4
  43.6 41.0 %reduce-scatter.9.cloned.1.call-start = ((), (), s32[]{:S(2)}) async-start(), calls=%async_computation.6 | async-start | bytes 286720 | tf_op jit(solution)/shard_map/reduce_scatter | solution.py:46
  44.6 77.7 %reduce-scatter.11.cloned.1.call-start = ((), (), s32[]{:S(2)}) async-start(), calls=%async_computation.7 | async-start | bytes 1032192 | tf_op jit(solution)/shard_map/reduce_scatter | solution.py:60
  88.5 68.4 %reduce-scatter.5.cloned.1.call-start = ((), (), s32[]{:S(2)}) async-start(), calls=%async_computation.4 | async-start | bytes 3145728 | tf_op jit(solution)/shard_map/reduce_scatter | solution.py:53
Sparse Core Ops, SparseCore 0:
  43.7 20.6 reduce-scatter.6
  66.8 17.7 reduce-scatter.8
  88.6 33.6 reduce-scatter.10
  125.0 31.7 reduce-scatter.4
where the time goes:
time: 164 us; the launch traced here: 163 us
  waiting for transfers between devices  102 us (62%)
  blocking collectives  29.8 us (18%)
  matrix products  16 us (10%)
  between operations  13.8 us (8%)
    reduce_scatter x1, waiting for transfers between devices, body(): lax.psum_scatter(input_term.astype(jnp.bfloat16), 'tensor', scatter_dimen...  34.5 us
    reduce_scatter x1, waiting for transfers between devices, body(): lax.psum_scatter(encoder_term.astype(jnp.bfloat16), ('tensor', 'section')...  31.5 us
    reduce_scatter x1, waiting for transfers between devices, body(): lax.psum_scatter(dkey_part.astype(jnp.bfloat16), 'seq', scatter_dimension...  19.7 us
    reduce_scatter x1, waiting for transfers between devices, body(): lax.psum_scatter(dvalue_part.astype(jnp.bfloat16), 'seq', scatter_dimensi...  16.5 us
    all_gather x1, blocking collectives, body(): lax.all_gather(key, 'seq', axis=0, tiled=True)  15.6 us
    all_gather x1, blocking collectives, body(): lax.all_gather(value, 'seq', axis=0, tiled=True)  14.2 us
    dot_general x1, matrix products, body(): jnp.einsum('kd,ed->ke', dvalue, wv_own, preferred_element_type=jnp.float32)  3.86 us
    dot_general x1, matrix products, body(): jnp.einsum('kd,ed->ke', dkey, wk_own, preferred_element_type=jnp.float32)  3.66 us
  transfers between devices with their start and end apart: 4, of which 4 were waited for; matrix products, arithmetic and copies ran while one was open for 4% of the time, Pallas kernels for 0%

commit v1 on v0

v1 whole, which is shorter than its diff:
```python
import functools
import math

import jax
import jax.numpy as jnp
from jax import lax
from jax.experimental import pallas as pl
from jax.experimental.pallas import tpu as pltpu
from jax.sharding import PartitionSpec as P

masked_fill = -1e30
f32 = jnp.float32
bf16 = jnp.bfloat16
MESH = pl.DeviceIdType.MESH


def nt(a, b):
    return lax.dot_general(a, b, (((1,), (1,)), ((), ())), preferred_element_type=f32)


def tn(a, b):
    return lax.dot_general(a, b, (((0,), (0,)), ((), ())), preferred_element_type=f32)


def kernel(
    S, T, C,
    len_ref, dec_hbm, wq_hbm, wk_hbm, wv_hbm, dout_hbm, enc_hbm,
    dec_out, enc_out,
    enc_v, wk_v, wv_v, dec_v, wq_v, dout_v,
    k_all, v_all, q_v, wq_recv, dq_v, dq_recv,
    sc_v, dp_v, ds_v, rs_send, rs_recv, own_kv,
    acc_v, dec_v_out, l1_send, l1_recv, l2_send, l2_recv, enc_v_out,
    load_sem, out_sem,
    wq_ss, wq_rs, k_ss, k_rs, v_ss, v_rs, dk_ss, dk_rs, dv_ss, dv_rs, dq_ss, dq_rs,
    l1_ss, l1_rs, l2_ss, l2_rs,
):
    s = lax.axis_index("seq")
    t = lax.axis_index("tensor")
    c = lax.axis_index("section")
    X = C // 2
    kd = enc_hbm.shape[0]
    D = enc_hbm.shape[1]
    half = D // T
    sl = D // (T * C)
    scale = 1.0 / math.sqrt(wq_hbm.shape[1])
    core = lax.rem(c, 2)
    partner = c + 1 - 2 * core

    def seq_peer(r):
        return {"seq": lax.rem(s + r, S)}

    def plane(i):
        return lax.rem(t + i // X, T), lax.rem(c + 2 * (i % X), C)

    def plane_peer(i):
        pt, pc = plane(i)
        return {"tensor": pt, "section": pc}

    barrier = pltpu.get_barrier_semaphore()
    for r in range(1, S):
        pl.semaphore_signal(barrier, inc=1, device_id=seq_peer(r), device_id_type=MESH)
    for i in range(1, T * X):
        pl.semaphore_signal(barrier, inc=1, device_id=plane_peer(i), device_id_type=MESH)
    pl.semaphore_signal(barrier, inc=1, device_id={"section": partner}, device_id_type=MESH)

    pairs = ((enc_hbm, enc_v), (wk_hbm, wk_v), (wv_hbm, wv_v), (dec_hbm, dec_v), (wq_hbm, wq_v), (dout_hbm, dout_v))
    loads = [pltpu.make_async_copy(a, b, load_sem.at[i]) for i, (a, b) in enumerate(pairs)]
    for l in loads:
        l.start()
    pl.semaphore_wait(barrier, (S - 1) + (T * X - 1) + 1)

    def remote(src, dst, ss, rs, dev):
        cp = pltpu.make_async_remote_copy(
            src_ref=src, dst_ref=dst, send_sem=ss, recv_sem=rs, device_id=dev, device_id_type=MESH
        )
        cp.start()
        return cp

    wq_cp = []
    for r in range(1, T):
        pt = lax.rem(t + r, T)
        rows = pl.ds(pl.multiple_of(pt * half, half), half)
        wq_cp.append(remote(wq_hbm.at[rows], wq_recv.at[r - 1], wq_ss.at[r - 1], wq_rs.at[r - 1], {"tensor": pt}))

    def block(b):
        return pl.ds(pl.multiple_of(b * kd, 16), kd)

    mine = block(s)
    loads[0].wait()
    loads[1].wait()
    k_all[mine] = jnp.dot(enc_v[...], wk_v[...], preferred_element_type=f32).astype(bf16)
    order = sorted(range(1, S), key=lambda r: -min(r, S - r))
    k_cp = {r: remote(k_all.at[mine], k_all.at[mine], k_ss.at[r - 1], k_rs.at[r - 1], seq_peer(r)) for r in order}
    loads[2].wait()
    v_all[mine] = jnp.dot(enc_v[...], wv_v[...], preferred_element_type=f32).astype(bf16)
    v_cp = {r: remote(v_all.at[mine], v_all.at[mine], v_ss.at[r - 1], v_rs.at[r - 1], seq_peer(r)) for r in order}

    loads[3].wait()
    loads[4].wait()
    q_v[...] = jnp.dot(dec_v[...], wq_v[...], preferred_element_type=f32).astype(bf16)
    loads[5].wait()

    slots = lax.broadcasted_iota(jnp.int32, (kd, q_v.shape[0]), 0)

    near = [0] + sorted(range(1, S), key=lambda r: min(r, S - r))
    top = None
    for r in near:
        b = lax.rem(s - r + S, S)
        if r:
            k_cp[r].wait_recv()
        sc = nt(k_all[block(b)], q_v[...]) * scale
        sc = jnp.where(slots < len_ref[b], sc, masked_fill)
        sc_v[block(b)] = sc
        m = jnp.max(sc, axis=0, keepdims=True)
        top = m if top is None else jnp.maximum(top, m)
    total = jnp.zeros_like(top)
    for b in range(S):
        e = jnp.where(slots < len_ref[b], jnp.exp(sc_v[block(b)] - top), 0.0)
        sc_v[block(b)] = e
        total = total + jnp.sum(e, axis=0, keepdims=True)
    inv = 1.0 / total
    delta = jnp.zeros_like(top)
    for r in near:
        b = lax.rem(s - r + S, S)
        if r:
            v_cp[r].wait_recv()
        dp = nt(v_all[block(b)], dout_v[...])
        dp_v[block(b)] = dp
        delta = delta + jnp.sum(sc_v[block(b)] * dp, axis=0, keepdims=True)
    delta = delta * inv

    dk_cp = {}
    dv_cp = {}
    for r in order + [0]:
        b = lax.rem(s + r, S)
        p = sc_v[block(b)] * inv
        ds = (p * (dp_v[block(b)] - delta) * scale).astype(bf16)
        ds_v[block(b)] = ds
        dk = jnp.dot(ds, q_v[...], preferred_element_type=f32)
        dv = jnp.dot(p.astype(bf16), dout_v[...], preferred_element_type=f32)
        if r:
            rs_send[r - 1, 0] = dk.astype(bf16)
            dk_cp[r] = remote(rs_send.at[r - 1, 0], rs_recv.at[r - 1, 0], dk_ss.at[r - 1], dk_rs.at[r - 1], seq_peer(r))
            rs_send[r - 1, 1] = dv.astype(bf16)
            dv_cp[r] = remote(rs_send.at[r - 1, 1], rs_recv.at[r - 1, 1], dv_ss.at[r - 1], dv_rs.at[r - 1], seq_peer(r))
        else:
            own_kv[0] = dk
            own_kv[1] = dv

    dq_v[...] = tn(ds_v[...], k_all[...]).astype(bf16)
    dq_cp = [
        remote(dq_v, dq_recv.at[r - 1], dq_ss.at[r - 1], dq_rs.at[r - 1], {"tensor": lax.rem(t + r, T)})
        for r in range(1, T)
    ]
    step = min(half, 512)
    for j in range(half // step):
        rows = pl.ds(pl.multiple_of(t * half + j * step, step), step)
        acc_v[:, j * step:(j + 1) * step] = nt(dq_v[...], wq_v[rows])

    for r in near[1:]:
        dk_cp[r].wait_recv()
        dv_cp[r].wait_recv()
    dkey = own_kv[0]
    dvalue = own_kv[1]
    for r in range(1, S):
        dkey = dkey + rs_recv[r - 1, 0].astype(f32)
        dvalue = dvalue + rs_recv[r - 1, 1].astype(f32)
    dkey = dkey.astype(bf16)
    dvalue = dvalue.astype(bf16)

    def enc_term(pt, pc):
        rows = pl.ds(pl.multiple_of((pt * C + pc) * sl, sl), sl)
        return nt(dkey, wk_v[rows]) + nt(dvalue, wv_v[rows])

    n2 = T * X
    far = list(range(n2 - 1, -1, -1))
    l1_cp = {}
    for i in far:
        pt, pc = plane(i)
        l1_send[i] = enc_term(pt, pc + 1 - 2 * core).astype(bf16)
        l1_cp[i] = remote(l1_send.at[i], l1_recv.at[i], l1_ss.at[i], l1_rs.at[i], {"section": partner})
    l2_cp = {}
    total_enc = None
    for i in far:
        pt, pc = plane(i)
        term = enc_term(pt, pc)
        l1_cp[i].wait_recv()
        term = term + l1_recv[i].astype(f32)
        if i:
            l2_send[i - 1] = term.astype(bf16)
            l2_cp[i] = remote(l2_send.at[i - 1], l2_recv.at[i - 1], l2_ss.at[i - 1], l2_rs.at[i - 1], plane_peer(i))
        else:
            total_enc = term

    for r in range(1, T):
        wq_cp[r - 1].wait_recv()
        dq_cp[r - 1].wait_recv()
    for j in range(half // step):
        cols = slice(j * step, (j + 1) * step)
        a = acc_v[:, cols]
        for r in range(1, T):
            a = a + nt(dq_recv[r - 1], wq_recv[r - 1, cols])
        dec_v_out[:, cols] = a.astype(bf16)
    dec_cp = pltpu.make_async_copy(dec_v_out, dec_out, out_sem.at[0])
    dec_cp.start()

    for i in range(1, n2):
        l2_cp[i].wait_recv()
        total_enc = total_enc + l2_recv[i - 1].astype(f32)
    enc_v_out[...] = total_enc.astype(bf16)
    enc_cp = pltpu.make_async_copy(enc_v_out, enc_out, out_sem.at[1])
    enc_cp.start()

    for cp in wq_cp + dq_cp + [d[k] for d in (k_cp, v_cp, dk_cp, dv_cp, l1_cp, l2_cp) for k in d]:
        cp.wait_send()
    dec_cp.wait()
    enc_cp.wait()


def body(S, T, C, dec_inputs, w_query, w_key, w_value, ctx_grad, encoded, enc_lengths):
    tq = dec_inputs.shape[1]
    kd, D = encoded.shape
    dh = w_query.shape[2]
    half, sl, X = D // T, D // (T * C), C // 2
    n2 = T * X
    V = pltpu.VMEM
    dma = pltpu.SemaphoreType.DMA
    hbm = pl.BlockSpec(memory_space=pl.ANY)
    out = pl.pallas_call(
        functools.partial(kernel, S, T, C),
        out_shape=(jax.ShapeDtypeStruct((tq, half), bf16), jax.ShapeDtypeStruct((kd, sl), bf16)),
        in_specs=[pl.BlockSpec(memory_space=pltpu.SMEM)] + [hbm] * 6,
        out_specs=(hbm, hbm),
        scratch_shapes=[
            V((kd, D), bf16), V((D, dh), bf16), V((D, dh), bf16), V((tq, D), bf16), V((D, dh), bf16), V((tq, dh), bf16),
            V((S * kd, dh), bf16), V((S * kd, dh), bf16), V((tq, dh), bf16),
            V((T - 1, half, dh), bf16), V((tq, dh), bf16), V((T - 1, tq, dh), bf16),
            V((S * kd, tq), f32), V((S * kd, tq), f32), V((S * kd, tq), bf16),
            V((S - 1, 2, kd, dh), bf16), V((S - 1, 2, kd, dh), bf16), V((2, kd, dh), f32),
            V((tq, half), f32), V((tq, half), bf16),
            V((n2, kd, sl), bf16), V((n2, kd, sl), bf16), V((n2 - 1, kd, sl), bf16), V((n2 - 1, kd, sl), bf16),
            V((kd, sl), bf16),
            dma((6,)), dma((2,)),
            dma((T - 1,)), dma((T - 1,)),
            dma((S - 1,)), dma((S - 1,)), dma((S - 1,)), dma((S - 1,)),
            dma((S - 1,)), dma((S - 1,)), dma((S - 1,)), dma((S - 1,)),
            dma((T - 1,)), dma((T - 1,)),
            dma((n2,)), dma((n2,)), dma((n2 - 1,)), dma((n2 - 1,)),
        ],
        compiler_params=pltpu.CompilerParams(
            collective_id=0, has_side_effects=True, vmem_limit_bytes=56 << 20
        ),
    )(enc_lengths, dec_inputs[0], w_query[0], w_key[0], w_value[0], ctx_grad[0], encoded)
    return (out[0][None, :, :], out[1])


def solution(mesh):
    in_specs = (
        P("section", "seq", None),
        P("section", None, "tensor"),
        P("section", None, "tensor"),
        P("section", None, "tensor"),
        P("section", "seq", "tensor"),
        P("seq", None),
        P(),
    )
    out_specs = (P("section", "seq", "tensor"), P("seq", ("tensor", "section")))
    f = functools.partial(body, mesh.shape["seq"], mesh.shape["tensor"], mesh.shape["section"])
    return jax.shard_map(f, mesh=mesh, in_specs=in_specs, out_specs=out_specs, check_vma=False)
```

time: 164 us -> 43 us (0.26)
  waiting for transfers between devices: 102 us -> 0 us
  Pallas kernels: 0 us -> 39.2 us
  blocking collectives: 29.8 us -> 0 us
  matrix products: 16 us -> 0 us
  between operations: 13.8 us -> 0.65 us
  local copies, waits for them, and re-layouts: 0.12 us -> 2.99 us
    reduce_scatter x4 -> x0, waiting for transfers between devices: 102 us -> none  [the longest x1 34.5 us: body(): lax.psum_scatter(input_term.astype(jnp.bfloat16), 'tensor', scatter_dimen...]
    pallas_call x0 -> x1, Pallas kernels: none -> 39.2 us  [body(): pl.pallas_call(functools.partial(kernel, S, T, C), out_shape=(jax.ShapeDt...]
    all_gather x2 -> x0, blocking collectives: 29.8 us -> none  [the longest x1 15.6 us: body(): lax.all_gather(key, 'seq', axis=0, tiled=True)]
    dot_general x10 -> x0, matrix products: 16 us -> none  [the longest x1 3.86 us: body(): jnp.einsum('kd,ed->ke', dvalue, wv_own, preferred_element_type=jnp.float32)]
    unnamed x10 -> x4, local copies, waits for them, and re-layouts: 0.03 us -> 2.99 us
  transfers between devices with their start and end apart: 4 -> 0, of which waited for: 4 -> 0; matrix products, arithmetic and copies ran while one was open for 4% -> 0% of each run, Pallas kernels for 0% -> 0%
where the time goes in v1:
time: 43 us; the launch traced here: 42.8 us
  Pallas kernels  39.2 us (91%)
  local copies, waits for them, and re-layouts  2.99 us (7%)
  between operations  0.65 us (2%)
    pallas_call x1, Pallas kernels, body(): pl.pallas_call(functools.partial(kernel, S, T, C), out_shape=(jax.ShapeDt...  39.2 us
    unnamed x4, local copies, waits for them, and re-layouts  2.99 us

profile of v1, /device:TPU:0, one launch (start us, length us, event | category | flops | bytes accessed | tf_op | source)
XLA Modules:
  0.0 42.8 jit_solution(13954820608834364069)
XLA Ops:
  0.6 39.2 %shard_map.86 = (bf16[256,2048]{1,0:T(8,128)(2,1)}, bf16[112,512]{1,0:T(8,128)(2,1)}) custom-call(s32[4]{0:T(128)} %len_ref.1, bf16[256,4096]{1,0:T(8,128)(2,1)} %bitcast.6, bf16[4096,256]{1,0:T(8,128)(2,1)} %bitcast.7, bf16[4096,256]{1,0:T(8,128)(2,1)} %bitcast.8, bf16[4096,256]{1,0:T(8,128)(2,1)} %bitcast.9, bf16[256,256]{1,0:T(8,128)(2,1)} %bitcast.11, ...), custom_call_target="tpu_custom_call" | custom-call | tf_op jit(solution)/shard_map/pallas_call | solution.py:229
  39.8 0.0 copy-start
  39.8 2.3 %copy.11 = bf16[1,256,2048]{2,1,0:T(8,128)(2,1)} copy(bf16[1,256,2048]{2,1,0:T(8,128)(2,1)} %bitcast.10) | data formatting | bytes 2097152
  42.2 0.0 copy-done
  42.2 0.6 %copy.12 = bf16[112,512]{1,0:T(8,128)(2,1)} copy(bf16[112,512]{1,0:T(8,128)(2,1)S(1)} %copy-done) | data formatting | bytes 229376
Async XLA Ops:
  39.8 2.4 %copy-start = (bf16[112,512]{1,0:T(8,128)(2,1)S(1)}, bf16[112,512]{1,0:T(8,128)(2,1)}, u32[]{:S(2)}) copy-start(bf16[112,512]{1,0:T(8,128)(2,1)} %get-tuple-element.9) | copy-start | bytes 344068

commit v2 on v1

--- a/solution.py
+++ b/solution.py
@@ -9,6 +9,7 @@
 from jax.sharding import PartitionSpec as P
 
 masked_fill = -1e30
+pieces = 4
 f32 = jnp.float32
 bf16 = jnp.bfloat16
 MESH = pl.DeviceIdType.MESH
@@ -29,8 +30,8 @@
     enc_v, wk_v, wv_v, dec_v, wq_v, dout_v,
     k_all, v_all, q_v, wq_recv, dq_v, dq_recv,
     sc_v, dp_v, ds_v, rs_send, rs_recv, own_kv,
-    acc_v, dec_v_out, l1_send, l1_recv, l2_send, l2_recv, enc_v_out,
-    load_sem, out_sem,
+    acc_v, term_v, l1_send, l1_recv, l2_send, l2_recv,
+    load_sem,
     wq_ss, wq_rs, k_ss, k_rs, v_ss, v_rs, dk_ss, dk_rs, dv_ss, dv_rs, dq_ss, dq_rs,
     l1_ss, l1_rs, l2_ss, l2_rs,
 ):
@@ -63,7 +64,13 @@
         pl.semaphore_signal(barrier, inc=1, device_id=plane_peer(i), device_id_type=MESH)
     pl.semaphore_signal(barrier, inc=1, device_id={"section": partner}, device_id_type=MESH)
 
-    pairs = ((enc_hbm, enc_v), (wk_hbm, wk_v), (wv_hbm, wv_v), (dec_hbm, dec_v), (wq_hbm, wq_v), (dout_hbm, dout_v))
+    piece = D // pieces
+    part = [pl.ds(i * piece, piece) for i in range(pieces)]
+    pairs = []
+    for p in part:
+        pairs.append((enc_hbm.at[:, p], enc_v.at[:, p]))
+        pairs.append((wk_hbm.at[p], wk_v.at[p]))
+    pairs += [(wv_hbm, wv_v), (dec_hbm, dec_v), (wq_hbm, wq_v), (dout_hbm, dout_v)]
     loads = [pltpu.make_async_copy(a, b, load_sem.at[i]) for i, (a, b) in enumerate(pairs)]
     for l in loads:
         l.start()
@@ -86,19 +93,23 @@
         return pl.ds(pl.multiple_of(b * kd, 16), kd)
 
     mine = block(s)
-    loads[0].wait()
-    loads[1].wait()
-    k_all[mine] = jnp.dot(enc_v[...], wk_v[...], preferred_element_type=f32).astype(bf16)
+    key = None
+    for i, p in enumerate(part):
+        loads[2 * i].wait()
+        loads[2 * i + 1].wait()
+        term = jnp.dot(enc_v[:, p], wk_v[p], preferred_element_type=f32)
+        key = term if key is None else key + term
+    k_all[mine] = key.astype(bf16)
     order = sorted(range(1, S), key=lambda r: -min(r, S - r))
     k_cp = {r: remote(k_all.at[mine], k_all.at[mine], k_ss.at[r - 1], k_rs.at[r - 1], seq_peer(r)) for r in order}
-    loads[2].wait()
+    loads[-4].wait()
     v_all[mine] = jnp.dot(enc_v[...], wv_v[...], preferred_element_type=f32).astype(bf16)
     v_cp = {r: remote(v_all.at[mine], v_all.at[mine], v_ss.at[r - 1], v_rs.at[r - 1], seq_peer(r)) for r in order}
 
-    loads[3].wait()
-    loads[4].wait()
+    loads[-3].wait()
+    loads[-2].wait()
     q_v[...] = jnp.dot(dec_v[...], wq_v[...], preferred_element_type=f32).astype(bf16)
-    loads[5].wait()
+    loads[-1].wait()
 
     slots = lax.broadcasted_iota(jnp.int32, (kd, q_v.shape[0]), 0)
 
@@ -119,6 +130,18 @@
         sc_v[block(b)] = e
         total = total + jnp.sum(e, axis=0, keepdims=True)
     inv = 1.0 / total
+    dk_cp = {}
+    dv_cp = {}
+    for r in order + [0]:
+        b = lax.rem(s + r, S)
+        p = sc_v[block(b)] * inv
+        sc_v[block(b)] = p
+        dv = jnp.dot(p.astype(bf16), dout_v[...], preferred_element_type=f32)
+        if r:
+            rs_send[r - 1, 1] = dv.astype(bf16)
+            dv_cp[r] = remote(rs_send.at[r - 1, 1], rs_recv.at[r - 1, 1], dv_ss.at[r - 1], dv_rs.at[r - 1], seq_peer(r))
+        else:
+            own_kv[1] = dv
     delta = jnp.zeros_like(top)
     for r in near:
         b = lax.rem(s - r + S, S)
@@ -127,25 +150,16 @@
         dp = nt(v_all[block(b)], dout_v[...])
         dp_v[block(b)] = dp
         delta = delta + jnp.sum(sc_v[block(b)] * dp, axis=0, keepdims=True)
-    delta = delta * inv
-
-    dk_cp = {}
-    dv_cp = {}
     for r in order + [0]:
         b = lax.rem(s + r, S)
-        p = sc_v[block(b)] * inv
-        ds = (p * (dp_v[block(b)] - delta) * scale).astype(bf16)
+        ds = (sc_v[block(b)] * (dp_v[block(b)] - delta) * scale).astype(bf16)
         ds_v[block(b)] = ds
         dk = jnp.dot(ds, q_v[...], preferred_element_type=f32)
-        dv = jnp.dot(p.astype(bf16), dout_v[...], preferred_element_type=f32)
         if r:
             rs_send[r - 1, 0] = dk.astype(bf16)
             dk_cp[r] = remote(rs_send.at[r - 1, 0], rs_recv.at[r - 1, 0], dk_ss.at[r - 1], dk_rs.at[r - 1], seq_peer(r))
-            rs_send[r - 1, 1] = dv.astype(bf16)
-            dv_cp[r] = remote(rs_send.at[r - 1, 1], rs_recv.at[r - 1, 1], dv_ss.at[r - 1], dv_rs.at[r - 1], seq_peer(r))
         else:
             own_kv[0] = dk
-            own_kv[1] = dv
 
     dq_v[...] = tn(ds_v[...], k_all[...]).astype(bf16)
     dq_cp = [
@@ -157,33 +171,39 @@
         rows = pl.ds(pl.multiple_of(t * half + j * step, step), step)
         acc_v[:, j * step:(j + 1) * step] = nt(dq_v[...], wq_v[rows])
 
+    n2 = T * X
+    far = list(range(n2 - 1, -1, -1))
+
+    def wrows(k, i):
+        pt, pc = plane(i)
+        pc = pc if k else pc + 1 - 2 * core
+        return pl.ds(pl.multiple_of((pt * C + pc) * sl, sl), sl)
+
+    dvalue = own_kv[1]
+    for r in near[1:]:
+        dv_cp[r].wait_recv()
+        dvalue = dvalue + rs_recv[r - 1, 1].astype(f32)
+    dvalue = dvalue.astype(bf16)
+    for k in range(2):
+        for i in far:
+            term_v[k, i] = nt(dvalue, wv_v[wrows(k, i)])
+    dkey = own_kv[0]
     for r in near[1:]:
         dk_cp[r].wait_recv()
-        dv_cp[r].wait_recv()
-    dkey = own_kv[0]
-    dvalue = own_kv[1]
-    for r in range(1, S):
         dkey = dkey + rs_recv[r - 1, 0].astype(f32)
-        dvalue = dvalue + rs_recv[r - 1, 1].astype(f32)
     dkey = dkey.astype(bf16)
-    dvalue = dvalue.astype(bf16)
-
-    def enc_term(pt, pc):
-        rows = pl.ds(pl.multiple_of((pt * C + pc) * sl, sl), sl)
-        return nt(dkey, wk_v[rows]) + nt(dvalue, wv_v[rows])
-
-    n2 = T * X
-    far = list(range(n2 - 1, -1, -1))
+
+    def enc_term(k, i):
+        return nt(dkey, wk_v[wrows(k, i)]) + term_v[k, i]
+
     l1_cp = {}
     for i in far:
-        pt, pc = plane(i)
-        l1_send[i] = enc_term(pt, pc + 1 - 2 * core).astype(bf16)
+        l1_send[i] = enc_term(0, i).astype(bf16)
         l1_cp[i] = remote(l1_send.at[i], l1_recv.at[i], l1_ss.at[i], l1_rs.at[i], {"section": partner})
     l2_cp = {}
     total_enc = None
     for i in far:
-        pt, pc = plane(i)
-        term = enc_term(pt, pc)
+        term = enc_term(1, i)
         l1_cp[i].wait_recv()
         term = term + l1_recv[i].astype(f32)
         if i:
@@ -200,21 +220,27 @@
         a = acc_v[:, cols]
         for r in range(1, T):
             a = a + nt(dq_recv[r - 1], wq_recv[r - 1, cols])
-        dec_v_out[:, cols] = a.astype(bf16)
-    dec_cp = pltpu.make_async_copy(dec_v_out, dec_out, out_sem.at[0])
-    dec_cp.start()
+        dec_out[:, cols] = a.astype(bf16)
 
     for i in range(1, n2):
         l2_cp[i].wait_recv()
         total_enc = total_enc + l2_recv[i - 1].astype(f32)
-    enc_v_out[...] = total_enc.astype(bf16)
-    enc_cp = pltpu.make_async_copy(enc_v_out, enc_out, out_sem.at[1])
-    enc_cp.start()
+    enc_out[...] = total_enc.astype(bf16)
 
     for cp in wq_cp + dq_cp + [d[k] for d in (k_cp, v_cp, dk_cp, dv_cp, l1_cp, l2_cp) for k in d]:
         cp.wait_send()
-    dec_cp.wait()
-    enc_cp.wait()
+
+
+def store(dec_v, enc_v, dec_hbm, enc_hbm, sem):
+    rows = dec_v.shape[0] // 4
+    copies = [pltpu.make_async_copy(enc_v, enc_hbm, sem.at[4])]
+    for i in range(4):
+        p = pl.ds(i * rows, rows)
+        copies.append(pltpu.make_async_copy(dec_v.at[p], dec_hbm.at[p], sem.at[i]))
+    for cp in copies:
+        cp.start()
+    for cp in copies:
+        cp.wait()
 
 
 def body(S, T, C, dec_inputs, w_query, w_key, w_value, ctx_grad, encoded, enc_lengths):
@@ -226,21 +252,21 @@
     V = pltpu.VMEM
     dma = pltpu.SemaphoreType.DMA
     hbm = pl.BlockSpec(memory_space=pl.ANY)
+    vmem = pl.BlockSpec(memory_space=pltpu.VMEM)
     out = pl.pallas_call(
         functools.partial(kernel, S, T, C),
-        out_shape=(jax.ShapeDtypeStruct((tq, half), bf16), jax.ShapeDtypeStruct((kd, sl), bf16)),
+        out_shape=(V((tq, half), bf16), V((kd, sl), bf16)),
         in_specs=[pl.BlockSpec(memory_space=pltpu.SMEM)] + [hbm] * 6,
-        out_specs=(hbm, hbm),
+        out_specs=(vmem, vmem),
         scratch_shapes=[
             V((kd, D), bf16), V((D, dh), bf16), V((D, dh), bf16), V((tq, D), bf16), V((D, dh), bf16), V((tq, dh), bf16),
             V((S * kd, dh), bf16), V((S * kd, dh), bf16), V((tq, dh), bf16),
             V((T - 1, half, dh), bf16), V((tq, dh), bf16), V((T - 1, tq, dh), bf16),
             V((S * kd, tq), f32), V((S * kd, tq), f32), V((S * kd, tq), bf16),
             V((S - 1, 2, kd, dh), bf16), V((S - 1, 2, kd, dh), bf16), V((2, kd, dh), f32),
-            V((tq, half), f32), V((tq, half), bf16),
+            V((tq, half), f32), V((2, n2, kd, sl), f32),
             V((n2, kd, sl), bf16), V((n2, kd, sl), bf16), V((n2 - 1, kd, sl), bf16), V((n2 - 1, kd, sl), bf16),
-            V((kd, sl), bf16),
-            dma((6,)), dma((2,)),
+            dma((2 * pieces + 4,)),
             dma((T - 1,)), dma((T - 1,)),
             dma((S - 1,)), dma((S - 1,)), dma((S - 1,)), dma((S - 1,)),
             dma((S - 1,)), dma((S - 1,)), dma((S - 1,)), dma((S - 1,)),
@@ -251,7 +277,14 @@
             collective_id=0, has_side_effects=True, vmem_limit_bytes=56 << 20
         ),
     )(enc_lengths, dec_inputs[0], w_query[0], w_key[0], w_value[0], ctx_grad[0], encoded)
-    return (out[0][None, :, :], out[1])
+    dec_grad, enc_grad = pl.pallas_call(
+        store,
+        out_shape=(jax.ShapeDtypeStruct((tq, half), bf16), jax.ShapeDtypeStruct((kd, sl), bf16)),
+        in_specs=[vmem, vmem],
+        out_specs=(hbm, hbm),
+        scratch_shapes=[dma((5,))],
+    )(*[pltpu.with_memory_space_constraint(o, pltpu.VMEM) for o in out])
+    return (dec_grad[None, :, :], enc_grad)
 
 
 def solution(mesh):

time: 43 us -> 40.5 us (0.942)
  local copies, waits for them, and re-layouts: 2.99 us -> 0 us
  Pallas kernels: 39.2 us -> 39.7 us
    unnamed x4 -> x0, local copies, waits for them, and re-layouts: 2.99 us -> none
    pallas_call x1 -> x2, Pallas kernels: 39.2 us -> 39.7 us  [the longest x1 38.6 us: body(): pl.pallas_call(functools.partial(kernel, S, T, C), out_shape=(V((tq, half...]
where the time goes in v2:
time: 40.5 us; the launch traced here: 40.3 us
  Pallas kernels  39.7 us (98%)
  between operations  0.64 us (2%)
    pallas_call x1, Pallas kernels, body(): pl.pallas_call(functools.partial(kernel, S, T, C), out_shape=(V((tq, half...  38.6 us
    pallas_call x1, Pallas kernels, body(): pl.pallas_call(store, out_shape=(jax.ShapeDtypeStruct((tq, half), bf16),...  1.04 us

profile of v2, /device:TPU:0, one launch (start us, length us, event | category | flops | bytes accessed | tf_op | source)
XLA Modules:
  0.0 40.3 jit_solution(9261177341926609481)
XLA Ops:
  0.6 38.6 %shard_map.86 = (bf16[256,2048]{1,0:T(8,128)(2,1)S(1)}, bf16[112,512]{1,0:T(8,128)(2,1)S(1)}) custom-call(s32[4]{0:T(128)} %len_ref.1, bf16[256,4096]{1,0:T(8,128)(2,1)} %bitcast.6, bf16[4096,256]{1,0:T(8,128)(2,1)} %bitcast.7, bf16[4096,256]{1,0:T(8,128)(2,1)} %bitcast.8, bf16[4096,256]{1,0:T(8,128)(2,1)} %bitcast.9, bf16[256,256]{1,0:T(8,128)(2,1)} %bitcast.10, ...), custom_call_target="tpu_custom_call" | custom-call | tf_op jit(solution)/shard_map/pallas_call | solution.py:256
  39.3 1.0 %shard_map.87 = (bf16[256,2048]{1,0:T(8,128)(2,1)}, bf16[112,512]{1,0:T(8,128)(2,1)}) custom-call(bf16[256,2048]{1,0:T(8,128)(2,1)S(1)} %get-tuple-element.6.dec_v, bf16[112,512]{1,0:T(8,128)(2,1)S(1)} %get-tuple-element.7.enc_v), custom_call_target="tpu_custom_call" | custom-call | tf_op jit(solution)/shard_map/pallas_call | solution.py:280

commit v3 on v2

--- a/solution.py
+++ b/solution.py
@@ -30,10 +30,10 @@
     enc_v, wk_v, wv_v, dec_v, wq_v, dout_v,
     k_all, v_all, q_v, wq_recv, dq_v, dq_recv,
     sc_v, dp_v, ds_v, rs_send, rs_recv, own_kv,
-    acc_v, term_v, l1_send, l1_recv, l2_send, l2_recv,
+    acc_v, term_v, l1_send, l1_recv, l2_send, l2_recv, l3_send, l3_recv,
     load_sem,
-    wq_ss, wq_rs, k_ss, k_rs, v_ss, v_rs, dk_ss, dk_rs, dv_ss, dv_rs, dq_ss, dq_rs,
-    l1_ss, l1_rs, l2_ss, l2_rs,
+    wq_ss, wq_rs, kv_ss, kv_rs, dk_ss, dk_rs, dv_ss, dv_rs, dq_ss, dq_rs,
+    l1_ss, l1_rs, l2_ss, l2_rs, l3_ss, l3_rs,
 ):
     s = lax.axis_index("seq")
     t = lax.axis_index("tensor")
@@ -53,15 +53,13 @@
     def plane(i):
         return lax.rem(t + i // X, T), lax.rem(c + 2 * (i % X), C)
 
-    def plane_peer(i):
-        pt, pc = plane(i)
-        return {"tensor": pt, "section": pc}
-
     barrier = pltpu.get_barrier_semaphore()
     for r in range(1, S):
         pl.semaphore_signal(barrier, inc=1, device_id=seq_peer(r), device_id_type=MESH)
-    for i in range(1, T * X):
-        pl.semaphore_signal(barrier, inc=1, device_id=plane_peer(i), device_id_type=MESH)
+    for r in range(1, T):
+        pl.semaphore_signal(barrier, inc=1, device_id={"tensor": lax.rem(t + r, T)}, device_id_type=MESH)
+    for r in range(1, X):
+        pl.semaphore_signal(barrier, inc=1, device_id={"section": lax.rem(c + 2 * r, C)}, device_id_type=MESH)
     pl.semaphore_signal(barrier, inc=1, device_id={"section": partner}, device_id_type=MESH)
 
     piece = D // pieces
@@ -74,7 +72,7 @@
     loads = [pltpu.make_async_copy(a, b, load_sem.at[i]) for i, (a, b) in enumerate(pairs)]
     for l in loads:
         l.start()
-    pl.semaphore_wait(barrier, (S - 1) + (T * X - 1) + 1)
+    pl.semaphore_wait(barrier, (S - 1) + (T - 1) + (X - 1) + 1)
 
     def remote(src, dst, ss, rs, dev):
         cp = pltpu.make_async_remote_copy(
@@ -101,10 +99,43 @@
         key = term if key is None else key + term
     k_all[mine] = key.astype(bf16)
     order = sorted(range(1, S), key=lambda r: -min(r, S - r))
-    k_cp = {r: remote(k_all.at[mine], k_all.at[mine], k_ss.at[r - 1], k_rs.at[r - 1], seq_peer(r)) for r in order}
+
+    stores = (k_all, v_all)
+
+    def hop(a, side, d):
+        b = s - d if side == 0 else s + d
+        to = lax.rem(s + 1, S) if side == 0 else lax.rem(s + S - 1, S)
+        return pltpu.make_async_remote_copy(
+            src_ref=stores[a].at[block(b)], dst_ref=stores[a].at[block(b)],
+            send_sem=kv_ss.at[a, side, d], recv_sem=kv_rs.at[a, side, d],
+            device_id={"seq": to}, device_id_type=MESH,
+        )
+
+    def sends(side, d):
+        if side == 0:
+            return jnp.logical_and(s >= d, s + 1 < S)
+        return jnp.logical_and(s + d < S, s > 0)
+
+    def send(a, d):
+        for side in range(2):
+            @pl.when(sends(side, d))
+            def _():
+                hop(a, side, d).start()
+
+    def receive(a, d):
+        for side in range(2):
+            @pl.when(s > d if side == 0 else s + d + 1 < S)
+            def _():
+                hop(a, side, d).wait_recv()
+            if d + 1 < S - 1:
+                @pl.when(sends(side, d + 1))
+                def _():
+                    hop(a, side, d + 1).start()
+
+    send(0, 0)
     loads[-4].wait()
     v_all[mine] = jnp.dot(enc_v[...], wv_v[...], preferred_element_type=f32).astype(bf16)
-    v_cp = {r: remote(v_all.at[mine], v_all.at[mine], v_ss.at[r - 1], v_rs.at[r - 1], seq_peer(r)) for r in order}
+    send(1, 0)
 
     loads[-3].wait()
     loads[-2].wait()
@@ -114,20 +145,23 @@
     slots = lax.broadcasted_iota(jnp.int32, (kd, q_v.shape[0]), 0)
 
     near = [0] + sorted(range(1, S), key=lambda r: min(r, S - r))
+    for d in range(S - 1):
+        receive(0, d)
+        if d < S - 2:
+            receive(1, d)
     top = None
-    for r in near:
-        b = lax.rem(s - r + S, S)
-        if r:
-            k_cp[r].wait_recv()
-        sc = nt(k_all[block(b)], q_v[...]) * scale
+    for b in range(S):
+        fixed = slice(b * kd, (b + 1) * kd)
+        sc = nt(k_all[fixed], q_v[...]) * scale
         sc = jnp.where(slots < len_ref[b], sc, masked_fill)
-        sc_v[block(b)] = sc
+        sc_v[fixed] = sc
         m = jnp.max(sc, axis=0, keepdims=True)
         top = m if top is None else jnp.maximum(top, m)
     total = jnp.zeros_like(top)
     for b in range(S):
-        e = jnp.where(slots < len_ref[b], jnp.exp(sc_v[block(b)] - top), 0.0)
-        sc_v[block(b)] = e
+        fixed = slice(b * kd, (b + 1) * kd)
+        e = jnp.where(slots < len_ref[b], jnp.exp(sc_v[fixed] - top), 0.0)
+        sc_v[fixed] = e
         total = total + jnp.sum(e, axis=0, keepdims=True)
     inv = 1.0 / total
     dk_cp = {}
@@ -142,14 +176,13 @@
             dv_cp[r] = remote(rs_send.at[r - 1, 1], rs_recv.at[r - 1, 1], dv_ss.at[r - 1], dv_rs.at[r - 1], seq_peer(r))
         else:
             own_kv[1] = dv
+    receive(1, S - 2)
     delta = jnp.zeros_like(top)
-    for r in near:
-        b = lax.rem(s - r + S, S)
-        if r:
-            v_cp[r].wait_recv()
-        dp = nt(v_all[block(b)], dout_v[...])
-        dp_v[block(b)] = dp
-        delta = delta + jnp.sum(sc_v[block(b)] * dp, axis=0, keepdims=True)
+    for b in range(S):
+        fixed = slice(b * kd, (b + 1) * kd)
+        dp = nt(v_all[fixed], dout_v[...])
+        dp_v[fixed] = dp
+        delta = delta + jnp.sum(sc_v[fixed] * dp, axis=0, keepdims=True)
     for r in order + [0]:
         b = lax.rem(s + r, S)
         ds = (sc_v[block(b)] * (dp_v[block(b)] - delta) * scale).astype(bf16)
@@ -172,7 +205,7 @@
         acc_v[:, j * step:(j + 1) * step] = nt(dq_v[...], wq_v[rows])
 
     n2 = T * X
-    far = list(range(n2 - 1, -1, -1))
+    far = sorted(range(n2), key=lambda i: (i % X == 0, i // X == 0))
 
     def wrows(k, i):
         pt, pc = plane(i)
@@ -201,16 +234,26 @@
         l1_send[i] = enc_term(0, i).astype(bf16)
         l1_cp[i] = remote(l1_send.at[i], l1_recv.at[i], l1_ss.at[i], l1_rs.at[i], {"section": partner})
     l2_cp = {}
-    total_enc = None
+    l3_cp = {}
     for i in far:
         term = enc_term(1, i)
         l1_cp[i].wait_recv()
         term = term + l1_recv[i].astype(f32)
-        if i:
-            l2_send[i - 1] = term.astype(bf16)
-            l2_cp[i] = remote(l2_send.at[i - 1], l2_recv.at[i - 1], l2_ss.at[i - 1], l2_rs.at[i - 1], plane_peer(i))
+        if i % X:
+            l2_send[i] = term.astype(bf16)
+            to = {"section": lax.rem(c + 2 * (i % X), C)}
+            l2_cp[i] = remote(l2_send.at[i], l2_recv.at[i], l2_ss.at[i], l2_rs.at[i], to)
         else:
-            total_enc = term
+            term_v[1, i] = term
+    for rt in list(range(T - 1, -1, -1)):
+        total_enc = term_v[1, rt * X]
+        for x in range(1, X):
+            l2_cp[rt * X + x].wait_recv()
+            total_enc = total_enc + l2_recv[rt * X + x].astype(f32)
+        if rt:
+            l3_send[rt - 1] = total_enc.astype(bf16)
+            to = {"tensor": lax.rem(t + rt, T)}
+            l3_cp[rt] = remote(l3_send.at[rt - 1], l3_recv.at[rt - 1], l3_ss.at[rt - 1], l3_rs.at[rt - 1], to)
 
     for r in range(1, T):
         wq_cp[r - 1].wait_recv()
@@ -222,13 +265,19 @@
             a = a + nt(dq_recv[r - 1], wq_recv[r - 1, cols])
         dec_out[:, cols] = a.astype(bf16)
 
-    for i in range(1, n2):
-        l2_cp[i].wait_recv()
-        total_enc = total_enc + l2_recv[i - 1].astype(f32)
+    for rt in range(1, T):
+        l3_cp[rt].wait_recv()
+        total_enc = total_enc + l3_recv[rt - 1].astype(f32)
     enc_out[...] = total_enc.astype(bf16)
 
-    for cp in wq_cp + dq_cp + [d[k] for d in (k_cp, v_cp, dk_cp, dv_cp, l1_cp, l2_cp) for k in d]:
+    for cp in wq_cp + dq_cp + [d[k] for d in (dk_cp, dv_cp, l1_cp, l2_cp, l3_cp) for k in d]:
         cp.wait_send()
+    for a in range(2):
+        for d in range(S - 1):
+            for side in range(2):
+                @pl.when(sends(side, d))
+                def _():
+                    hop(a, side, d).wait_send()
 
 
 def store(dec_v, enc_v, dec_hbm, enc_hbm, sem):
@@ -265,13 +314,14 @@
             V((S * kd, tq), f32), V((S * kd, tq), f32), V((S * kd, tq), bf16),
             V((S - 1, 2, kd, dh), bf16), V((S - 1, 2, kd, dh), bf16), V((2, kd, dh), f32),
             V((tq, half), f32), V((2, n2, kd, sl), f32),
-            V((n2, kd, sl), bf16), V((n2, kd, sl), bf16), V((n2 - 1, kd, sl), bf16), V((n2 - 1, kd, sl), bf16),
+            V((n2, kd, sl), bf16), V((n2, kd, sl), bf16), V((n2, kd, sl), bf16), V((n2, kd, sl), bf16),
+            V((T - 1, kd, sl), bf16), V((T - 1, kd, sl), bf16),
             dma((2 * pieces + 4,)),
             dma((T - 1,)), dma((T - 1,)),
-            dma((S - 1,)), dma((S - 1,)), dma((S - 1,)), dma((S - 1,)),
+            dma((2, 2, S - 1)), dma((2, 2, S - 1)),
             dma((S - 1,)), dma((S - 1,)), dma((S - 1,)), dma((S - 1,)),
             dma((T - 1,)), dma((T - 1,)),
-            dma((n2,)), dma((n2,)), dma((n2 - 1,)), dma((n2 - 1,)),
+            dma((n2,)), dma((n2,)), dma((n2,)), dma((n2,)), dma((T - 1,)), dma((T - 1,)),
         ],
         compiler_params=pltpu.CompilerParams(
             collective_id=0, has_side_effects=True, vmem_limit_bytes=56 << 20

time: 40.5 us -> 38.7 us (0.956)
  Pallas kernels: 39.7 us -> 37.9 us
    pallas_call x1, Pallas kernels: 38.6 us -> 36.9 us  [body(): pl.pallas_call(functools.partial(kernel, S, T, C), out_shape=(V((tq, half...]
where the time goes in v3:
time: 38.7 us; the launch traced here: 38.5 us
  Pallas kernels  37.9 us (98%)
  between operations  0.64 us (2%)
    pallas_call x1, Pallas kernels, body(): pl.pallas_call(functools.partial(kernel, S, T, C), out_shape=(V((tq, half...  36.9 us
    pallas_call x1, Pallas kernels, body(): pl.pallas_call(store, out_shape=(jax.ShapeDtypeStruct((tq, half), bf16),...  1.04 us

profile of v3, /device:TPU:0, one launch (start us, length us, event | category | flops | bytes accessed | tf_op | source)
XLA Modules:
  0.0 38.5 jit_solution(8890098675254995669)
XLA Ops:
  0.6 36.9 %shard_map.86 = (bf16[256,2048]{1,0:T(8,128)(2,1)S(1)}, bf16[112,512]{1,0:T(8,128)(2,1)S(1)}) custom-call(s32[4]{0:T(128)} %len_ref.1, bf16[256,4096]{1,0:T(8,128)(2,1)} %bitcast.6, bf16[4096,256]{1,0:T(8,128)(2,1)} %bitcast.7, bf16[4096,256]{1,0:T(8,128)(2,1)} %bitcast.8, bf16[4096,256]{1,0:T(8,128)(2,1)} %bitcast.9, bf16[256,256]{1,0:T(8,128)(2,1)} %bitcast.10, ...), custom_call_target="tpu_custom_call" | custom-call | tf_op jit(solution)/shard_map/pallas_call | solution.py:305
  37.5 1.0 %shard_map.87 = (bf16[256,2048]{1,0:T(8,128)(2,1)}, bf16[112,512]{1,0:T(8,128)(2,1)}) custom-call(bf16[256,2048]{1,0:T(8,128)(2,1)S(1)} %get-tuple-element.6.dec_v, bf16[112,512]{1,0:T(8,128)(2,1)S(1)} %get-tuple-element.7.enc_v), custom_call_target="tpu_custom_call" | custom-call | tf_op jit(solution)/shard_map/pallas_call | solution.py:330
